TPU v7x, 256 devices: a whole 4x4x8 slice. The times are simulated.
256 devices in a mesh: layer: 64 (over y, x_lo, z), feat: 4 (over x_hi, core).
Axes of the slice: x: 4 (x_hi: 2, x_lo: 2; x = x_hi * 2 + x_lo), y: 4, z: 8, core: 2. Of those that a mesh axis runs over, the one named last changes fastest.
Arguments:
- sources: bfloat16 [256, 8192], P(('layer', 'feat')), may hold values from -6 to 6
- targets: bfloat16 [256, 16384], P(('layer', 'feat')), may hold values from -16 to 16
- enc_weight: bfloat16 [8192, 32768], P(None, ('feat', 'layer')), may hold values from -0.0625 to 0.0625
- enc_bias: float32 [32768], P(('feat', 'layer')), may hold values from -3 to 3
- dec_weight: bfloat16 [32768, 16384], P('feat', 'layer'), may hold values from -0.03125 to 0.03125
- dec_bias: float32 [16384], P('layer'), may hold values from -3 to 3
Outputs:
- enc_grad: bfloat16 [8192, 32768], P(None, ('feat', 'layer'))
- dec_grad: bfloat16 [32768, 16384], P('feat', 'layer')
- mse: float32 [], replicated
All inputs are finite; a program needn't handle non-finite values.
Results may differ from a plain program's by a relative error of at most 0.011.
Values may be sent and summed in bfloat16 or wider, within the bound.
No kernel may reach another device: no remote copies, remote signals or barrier semaphores. Data moves between devices by JAX's collectives and lax.ppermute only.
A program may use at most 128 MiB of HBM per device.

v0:
```python
import math
import jax
import jax.numpy as jnp
from jax import lax
from jax.sharding import PartitionSpec as P


def per_device(sources, targets, enc_weight, enc_bias, dec_weight, dec_bias):
    inputs = lax.all_gather(sources, ("layer", "feat"), axis=0, tiled=True)
    tokens = inputs.shape[0]
    preact = jnp.dot(inputs, enc_weight, preferred_element_type=jnp.float32) + enc_bias
    feats = jax.nn.gelu(preact).astype(jnp.bfloat16)
    n_layer = lax.axis_size("layer")
    width = dec_weight.shape[1]
    spread = lax.all_gather(targets, "feat", axis=0, tiled=True)
    blocks = spread.reshape(spread.shape[0], n_layer, width)
    owned = lax.all_to_all(blocks, "layer", split_axis=1, concat_axis=0, tiled=True)
    wanted = owned.reshape(tokens, width)
    all_feats = lax.all_gather(feats, "layer", axis=1, tiled=True)
    partial_value = jnp.dot(all_feats, dec_weight, preferred_element_type=jnp.float32)
    factor = 1.0 / math.sqrt(tokens)
    outputs = lax.psum(partial_value.astype(jnp.bfloat16), "feat").astype(jnp.float32) + dec_bias
    misfit = outputs - wanted.astype(jnp.float32)
    errors = (misfit * factor).astype(jnp.bfloat16)
    total_sq = lax.psum(jnp.sum(misfit * misfit), "layer")
    mse = total_sq / (tokens * n_layer * width)
    dec_grad = lax.dot_general(
        all_feats, errors, (((0,), (0,)), ((), ())), preferred_element_type=jnp.float32
    ).astype(jnp.bfloat16)
    grad_rows = lax.psum_scatter(
        lax.dot_general(
            dec_weight, errors, (((1,), (1,)), ((), ())), preferred_element_type=jnp.float32
        ),
        "layer",
        scatter_dimension=0,
        tiled=True,
    )
    feat_grad = grad_rows.T
    _, pullback = jax.vjp(jax.nn.gelu, preact)
    pre_grad = pullback(feat_grad)[0].astype(jnp.bfloat16)
    enc_grad = lax.dot_general(
        inputs, pre_grad, (((0,), (0,)), ((), ())), preferred_element_type=jnp.float32
    ).astype(jnp.bfloat16)
    return (enc_grad, dec_grad, mse)


def solution(mesh):
    return jax.shard_map(
        per_device,
        mesh=mesh,
        in_specs=(
            P(("layer", "feat"), None),
            P(("layer", "feat"), None),
            P(None, ("feat", "layer")),
            P(("feat", "layer")),
            P("feat", "layer"),
            P("layer"),
        ),
        out_specs=(P(None, ("feat", "layer")), P("feat", "layer"), P()),
        check_vma=False,
    )
```

profile of v0, /device:TPU:4, one launch (start us, length us, event | category | flops | bytes accessed | tf_op | source)
XLA Modules:
  0.0 1093.3 jit_solution(547445359311050839)
XLA Ops:
  7.2 0.0 copy-start
  7.2 0.0 copy-start.1
  7.2 0.0 all-gather.7.cloned.1.call-start
  7.2 0.7 all-gather.7.cloned.1.call-update
  7.9 0.0 all-gather.5.cloned.1.call-start
  8.0 423.7 %all-gather.7.cloned.1.call-done = bf16[256,1,8192]{2,1,0:T(2,128)(2,1)} async-done(((bf16[1,1,8192]{2,1,0:T(2,128)(2,1)}), bf16[256,1,8192]{2,1,0:T(2,128)(2,1)}) %all-gather.7.cloned.1.call-update) | async-done | bytes 4194320 | tf_op jit(solution)/shard_map/all_gather | solution.py:9
  431.6 0.0 copy-done
  431.6 8.9 multiply_convert_fusion.1
  440.6 0.0 all-gather.5.cloned.1.call-update
  440.6 0.0 copy-done.1
  440.6 7.3 all-gather.1
  447.9 1.5 reduce
  449.3 7.6 all-to-all-start
  457.0 0.0 copy-start.2
  457.0 0.0 all-reduce.2.cloned.1.call-start
  457.0 224.1 %all-gather.5.cloned.1.call-done = bf16[256,8192]{1,0:T(8,128)(2,1)} async-done(((bf16[256,128]{1,0:T(8,128)(2,1)}), bf16[256,8192]{1,0:T(8,128)(2,1)}) %all-gather.5.cloned.1.call-update) | async-done | bytes 4194320 | tf_op jit(solution)/shard_map/all_gather | solution.py:19
  681.1 5.4 convolution_convert_fusion.2
  686.5 0.0 all-reduce.2.cloned.1.call-update
  686.5 0.0 reduce-scatter.2.cloned.1.call-start
  686.6 0.0 all-to-all-done
  686.6 0.1 reshape.18
  686.7 40.1 %all-reduce.2.cloned.1.call-done = bf16[256,256]{1,0:T(8,128)(2,1)} async-done(((bf16[256,256]{1,0:T(8,128)(2,1)}), bf16[256,256]{1,0:T(8,128)(2,1)}) %all-reduce.2.cloned.1.call-update) | async-done | bytes 131088 | tf_op jit(solution)/shard_map/psum | solution.py:22
  726.8 0.0 copy-done.2
  726.8 1.6 multiply_reduce_fusion
  728.4 6.7 convolution_bitcast_fusion
  735.1 0.0 reduce-scatter.2.cloned.1.call-update
  735.1 160.3 %psum.15 = f32[]{:T(128)} all-reduce(f32[]{:T(128)} %get-tuple-element.12), channel_id=1, replica_groups=mesh['layer'=64,'feat'=4] {'layer'}, use_global_device_ids=true, to_apply=%region_3.0 | all-reduce | flops 1 | bytes 8 | tf_op jit(solution)/shard_map/psum | solution.py:25
  896.1 5.5 convolution_convert_fusion
  901.7 170.2 %reduce-scatter.2.cloned.1.call-done = f32[128,256]{0,1:T(8,128)} async-done(((f32[8192,256]{0,1:T(8,128)}), f32[128,256]{0,1:T(8,128)}) %reduce-scatter.2.cloned.1.call-update) | async-done | bytes 131088 | tf_op jit(solution)/shard_map/reduce_scatter | solution.py:30
  1071.8 9.8 fusion
  1081.6 4.1 copy.13
  (1 shorter events, 0.0 us)
Async XLA Ops:
  7.2 424.5 %copy-start = (bf16[8192,128]{1,0:T(8,128)(2,1)S(1)}, bf16[8192,128]{1,0:T(8,128)(2,1)}, u32[]{:S(2)}) copy-start(bf16[8192,128]{1,0:T(8,128)(2,1)} %param.8) | copy-start | bytes 6291460
  7.2 433.4 %copy-start.1 = (bf16[1,16384]{1,0:T(2,128)(2,1)S(1)}, bf16[1,16384]{1,0:T(2,128)(2,1)}, u32[]{:S(2)}) copy-start(bf16[1,16384]{1,0:T(2,128)(2,1)} %param.7) | copy-start | bytes 98308
  7.2 424.4 %all-gather.7.cloned.1.call-start = ((), (), s32[]{:S(2)}) async-start(), calls=%async_computation.5 | async-start | bytes 8421376 | tf_op jit(solution)/shard_map/all_gather | solution.py:9
  7.9 673.2 %all-gather.5.cloned.1.call-start = ((), (), s32[]{:S(2)}) async-start(), calls=%async_computation.2 | async-start | bytes 4259840 | tf_op jit(solution)/shard_map/all_gather | solution.py:19
  449.3 237.3 %all-to-all-start = ((bf16[4,64,256]{2,0,1:T(4,128)(2,1)}), bf16[4,64,256]{2,0,1:T(4,128)(2,1)S(1)}, u32[]{:S(2)}, u32[]{:S(2)}) async-start(bf16[4,64,256]{2,0,1:T(4,128)(2,1)} %bitcast.9), calls=%async_computation | async-start | bytes 262144 | tf_op jit(solution)/shard_map/all_to_all | solution.py:17
  457.0 269.9 %copy-start.2 = (f32[256]{0:T(256)S(1)}, f32[256]{0:T(256)}, u32[]{:S(2)}) copy-start(f32[256]{0:T(256)} %param.11) | copy-start | bytes 3076
  457.0 269.8 %all-reduce.2.cloned.1.call-start = ((), (), s32[]{:S(2)}) async-start(), calls=%async_computation.3 | async-start | bytes 262144 | tf_op jit(solution)/shard_map/psum | solution.py:22
  686.5 385.3 %reduce-scatter.2.cloned.1.call-start = ((), (), s32[]{:S(2)}) async-start(), calls=%async_computation.4 | async-start | bytes 8519680 | tf_op jit(solution)/shard_map/reduce_scatter | solution.py:30
Sparse Core Ops, SparseCore 0:
  9.9 421.7 all-gather.6
  440.7 240.4 all-gather.4
  686.7 40.1 all-reduce.1
  735.3 336.4 reduce-scatter.1
where the time goes:
time: 1090 us
  waiting for transfers between devices  859 us (79%)
  blocking collectives  168 us (15%)
  matrix products  36.3 us (3%)
  between operations  15.6 us (1%)
    all_gather x1, waiting for transfers between devices, per_device(): inputs = lax.all_gather(sources, ('layer', 'feat'), axis=0, tiled=True)  424 us
    all_gather x1, waiting for transfers between devices, per_device(): all_feats = lax.all_gather(feats, 'layer', axis=1, tiled=True)  224 us
    reduce_scatter x1, waiting for transfers between devices, per_device(): lax.psum_scatter(lax.dot_general(dec_weight, errors, (((1,), (1,)), ((),...  170 us
    psum x1, blocking collectives, per_device(): total_sq = lax.psum(jnp.sum(misfit * misfit), 'layer')  160 us
    psum x1, waiting for transfers between devices, per_device(): lax.psum(partial_value.astype(jnp.bfloat16), 'feat').astype(jnp.float32)  40.1 us
  transfers between devices with their start and end apart: 5, of which 4 were waited for; matrix products, arithmetic and copies ran while one was open for 1% of the time, Pallas kernels for 0%

commit v1 on v0

--- a/solution.py
+++ b/solution.py
@@ -16,7 +16,8 @@
     blocks = spread.reshape(spread.shape[0], n_layer, width)
     owned = lax.all_to_all(blocks, "layer", split_axis=1, concat_axis=0, tiled=True)
     wanted = owned.reshape(tokens, width)
-    all_feats = lax.all_gather(feats, "layer", axis=1, tiled=True)
+    outgoing = jnp.stack([feats] * lax.axis_size("layer"))
+    all_feats = jnp.concatenate(lax.all_to_all(outgoing, "layer", 0, 0), axis=1)
     partial_value = jnp.dot(all_feats, dec_weight, preferred_element_type=jnp.float32)
     factor = 1.0 / math.sqrt(tokens)
     outputs = lax.psum(partial_value.astype(jnp.bfloat16), "feat").astype(jnp.float32) + dec_bias

time: 1090 us -> 967 us (0.89)
  waiting for transfers between devices: 859 us -> 717 us
    all_gather x1 -> x0, waiting for transfers between devices: 224 us -> none  [per_device(): all_feats = lax.all_gather(feats, 'layer', axis=1, tiled=True)]
    all_to_all x0 -> x1, waiting for transfers between devices: none -> 78.6 us  [per_device(): all_feats = jnp.concatenate(lax.all_to_all(outgoing, 'layer', 0, 0), axis=1)]
  transfers between devices with their start and end apart: 5 -> 5, of which waited for: 4 -> 5; matrix products, arithmetic and copies ran while one was open for 1% -> 1% of each run, Pallas kernels for 0% -> 0%
where the time goes in v1:
time: 967 us
  waiting for transfers between devices  717 us (74%)
  blocking collectives  173 us (18%)
  matrix products  35.7 us (4%)
  between operations  15.6 us (2%)
  starting transfers between devices  15.5 us (2%)
    all_gather x1, waiting for transfers between devices, per_device(): inputs = lax.all_gather(sources, ('layer', 'feat'), axis=0, tiled=True)  424 us
    reduce_scatter x1, waiting for transfers between devices, per_device(): lax.psum_scatter(lax.dot_general(dec_weight, errors, (((1,), (1,)), ((),...  170 us
    psum x1, blocking collectives, per_device(): total_sq = lax.psum(jnp.sum(misfit * misfit), 'layer')  160 us
    all_to_all x1, waiting for transfers between devices, per_device(): all_feats = jnp.concatenate(lax.all_to_all(outgoing, 'layer', 0, 0), axis=1)  78.6 us
    psum x1, waiting for transfers between devices, per_device(): lax.psum(partial_value.astype(jnp.bfloat16), 'feat').astype(jnp.float32)  38.4 us
  transfers between devices with their start and end apart: 5, of which 5 were waited for; matrix products, arithmetic and copies ran while one was open for 1% of the time, Pallas kernels for 0%

profile of v1, /device:TPU:4, one launch (start us, length us, event | category | flops | bytes accessed | tf_op | source)
XLA Modules:
  0.0 966.6 jit_solution(5997116779071456082)
XLA Ops:
  7.2 0.0 copy-start
  7.2 0.0 all-gather.4.cloned.1.call-start
  7.2 0.7 all-gather.4.cloned.1.call-update
  7.9 423.7 %all-gather.4.cloned.1.call-done = bf16[256,1,8192]{2,1,0:T(2,128)(2,1)} async-done(((bf16[1,1,8192]{2,1,0:T(2,128)(2,1)}), bf16[256,1,8192]{2,1,0:T(2,128)(2,1)}) %all-gather.4.cloned.1.call-update) | async-done | bytes 4194320 | tf_op jit(solution)/shard_map/all_gather | solution.py:9
  431.6 0.0 copy-done
  431.6 8.3 multiply_convert_fusion.1
  439.9 0.1 copy.13
  440.0 2.5 stack.2
  442.5 0.0 copy-start.1
  442.5 8.0 all-to-all-start
  450.6 0.0 copy-done.1
  450.6 12.4 %all-gather.1 = bf16[4,1,16384]{2,1,0:T(2,128)(2,1)S(1)} all-gather(bf16[1,1,16384]{2,1,0:T(2,128)(2,1)S(1)} %bitcast.47), channel_id=1, replica_groups=mesh['layer'=64,'feat'=4] {'feat'}, dimensions={0}, use_global_device_ids=true | all-gather | bytes 163840 | tf_op jit(solution)/shard_map/all_gather | solution.py:15
  463.0 1.5 reduce
  464.4 78.6 %all-to-all-done = bf16[64,256,128]{1,2,0:T(8,128)(2,1)} async-done(((bf16[64,256,128]{1,2,0:T(8,128)(2,1)}), bf16[64,256,128]{1,2,0:T(8,128)(2,1)}, u32[]{:S(2)}, u32[]{:S(2)}) %all-to-all-start) | async-done | bytes 4194336 | tf_op jit(solution)/shard_map/all_to_all | solution.py:20
  543.0 7.4 all-to-all-start.1
  550.4 0.0 all-reduce.2.cloned.1.call-start
  550.4 0.0 copy-start.2
  550.5 5.4 convolution_convert_fusion.2
  555.9 0.0 all-reduce.2.cloned.1.call-update
  555.9 0.0 reduce-scatter.2.cloned.1.call-start
  556.0 5.6 all-to-all-done.1
  561.6 0.1 reshape.28
  561.7 38.4 %all-reduce.2.cloned.1.call-done = bf16[256,256]{1,0:T(8,128)(2,1)} async-done(((bf16[256,256]{1,0:T(8,128)(2,1)}), bf16[256,256]{1,0:T(8,128)(2,1)}) %all-reduce.2.cloned.1.call-update) | async-done | bytes 131088 | tf_op jit(solution)/shard_map/psum | solution.py:23
  600.1 0.0 copy-done.2
  600.1 1.6 multiply_reduce_fusion
  601.7 6.7 convolution_bitcast_fusion
  608.4 0.0 reduce-scatter.2.cloned.1.call-update
  608.4 160.3 %psum.15 = f32[]{:T(128)} all-reduce(f32[]{:T(128)} %get-tuple-element.12), channel_id=1, replica_groups=mesh['layer'=64,'feat'=4] {'layer'}, use_global_device_ids=true, to_apply=%region_3.0 | all-reduce | flops 1 | bytes 8 | tf_op jit(solution)/shard_map/psum | solution.py:26
  769.4 5.5 convolution_convert_fusion
  774.8 170.3 %reduce-scatter.2.cloned.1.call-done = f32[128,256]{0,1:T(8,128)} async-done(((f32[8192,256]{0,1:T(8,128)}), f32[128,256]{0,1:T(8,128)}) %reduce-scatter.2.cloned.1.call-update) | async-done | bytes 131088 | tf_op jit(solution)/shard_map/reduce_scatter | solution.py:31
  945.1 9.8 %fusion = bf16[8192,128]{0,1:T(8,128)(2,1)} fusion(bf16[256,1,8192]{2,1,0:T(2,128)(2,1)} %all-gather.4.cloned.1.call-done, f32[256,128]{1,0:T(8,128)S(1)} %get-tuple-element.15, f32[128,256]{0,1:T(8,128)} %reduce-scatter.2.cloned.1.call-done), kind=kOutput, calls=%fused_computation.3 | convolution fusion | flops 538574848 | bytes 6553600 | tf_op jit(solution)/shard_map/dot_general | solution.py:42
  954.9 4.1 copy.15
  (1 shorter events, 0.0 us)
Async XLA Ops:
  7.2 424.5 %copy-start = (bf16[8192,128]{1,0:T(8,128)(2,1)S(1)}, bf16[8192,128]{1,0:T(8,128)(2,1)}, u32[]{:S(2)}) copy-start(bf16[8192,128]{1,0:T(8,128)(2,1)} %param.8) | copy-start | bytes 6291460
  7.2 424.4 %all-gather.4.cloned.1.call-start = ((), (), s32[]{:S(2)}) async-start(), calls=%async_computation.5 | async-start | bytes 8421376 | tf_op jit(solution)/shard_map/all_gather | solution.py:9
  442.5 8.0 copy-start.1
  442.5 100.5 %all-to-all-start = ((bf16[64,256,128]{1,2,0:T(8,128)(2,1)}), bf16[64,256,128]{1,2,0:T(8,128)(2,1)}, u32[]{:S(2)}, u32[]{:S(2)}) async-start(bf16[64,256,128]{1,2,0:T(8,128)(2,1)} %stack.2), calls=%async_computation | async-start | bytes 8388608 | tf_op jit(solution)/shard_map/all_to_all | solution.py:20
  543.0 18.5 %all-to-all-start.1 = ((bf16[4,64,256]{2,0,1:T(4,128)(2,1)}), bf16[4,64,256]{2,0,1:T(4,128)(2,1)S(1)}, u32[]{:S(2)}, u32[]{:S(2)}) async-start(bf16[4,64,256]{2,0,1:T(4,128)(2,1)} %bitcast.12), calls=%async_computation.1 | async-start | bytes 262144 | tf_op jit(solution)/shard_map/all_to_all | solution.py:17
  550.4 49.7 %all-reduce.2.cloned.1.call-start = ((), (), s32[]{:S(2)}) async-start(), calls=%async_computation.3 | async-start | bytes 262144 | tf_op jit(solution)/shard_map/psum | solution.py:23
  550.4 49.6 %copy-start.2 = (f32[256]{0:T(256)S(1)}, f32[256]{0:T(256)}, u32[]{:S(2)}) copy-start(f32[256]{0:T(256)} %param.11) | copy-start | bytes 3076
  555.9 389.2 %reduce-scatter.2.cloned.1.call-start = ((), (), s32[]{:S(2)}) async-start(), calls=%async_computation.4 | async-start | bytes 8519680 | tf_op jit(solution)/shard_map/reduce_scatter | solution.py:31
Sparse Core Ops, SparseCore 0:
  9.9 421.7 all-gather.3
  556.0 44.0 all-reduce.1
  608.5 336.5 reduce-scatter.1
